TPU v7x, 512 devices: a whole 4x4x16 slice. The times are simulated.
512 devices in a mesh: section: 4 (over x), dp: 16 (over z), expert: 8 (over y, core).
Axes of the slice: x: 4, y: 4, z: 16, core: 2. Of those that a mesh axis runs over, the one named last changes fastest.
Arguments:
- section_input: bfloat16 [4, 16384, 1024], P('section', ('dp', 'expert')), may hold values from -6 to 6
- saved_input: bfloat16 [4, 16384, 1024], P('section', ('dp', 'expert')), may hold values from -6 to 6
- cotangent: bfloat16 [4, 16384, 1024], P('section', ('dp', 'expert')), may hold values from -6 to 6
- routes_forward: int32 [4, 16384, 8], P('section', ('dp', 'expert')), may hold values from 0 to 63, as said below
- gates_forward: float32 [4, 16384, 8], P('section', ('dp', 'expert')), may hold values from 0.5 to 2
- routes_backward: int32 [4, 16384, 8], P('section', ('dp', 'expert')), may hold values from 0 to 63, as said below
- gates_backward: float32 [4, 16384, 8], P('section', ('dp', 'expert')), may hold values from 0.5 to 2
- gate_weight: bfloat16 [4, 8, 1024, 512], P('section', 'expert', 'dp'), may hold values from -0.1875 to 0.1875
- up_weight: bfloat16 [4, 8, 1024, 512], P('section', 'expert', 'dp'), may hold values from -0.1875 to 0.1875
- down_weight: bfloat16 [4, 8, 512, 1024], P('section', 'expert', 'dp'), may hold values from -0.25 to 0.25
Outputs:
- handed: bfloat16 [4, 16384, 1024], P('section', ('dp', 'expert'))
- grad_back: bfloat16 [4, 16384, 1024], P('section', ('dp', 'expert'))
- grad_gate: float32 [4, 8, 1024, 512], P('section', 'expert', 'dp')
- grad_up: float32 [4, 8, 1024, 512], P('section', 'expert', 'dp')
- grad_down: float32 [4, 8, 512, 1024], P('section', 'expert', 'dp')
Inputs may be any that keep to these rules, and one draw needn't show every extreme that they name: `routes_forward`: each token names 8 different experts. In every layer, every block of 128 tokens of one device names each expert below 8 between 1 and 32 times, and in every layer some expert below 8 is named exactly 32 times by every block. `routes_backward`: as routes_forward.
All inputs are finite; a program needn't handle non-finite values.
Results may differ from a plain program's by a relative error of at most 0.017.
Values may be sent and summed in bfloat16 or wider, within the bound.
No kernel may reach another device: no remote copies, remote signals or barrier semaphores. Data moves between devices by JAX's collectives and lax.ppermute only.
A program may use at most 64 MiB of HBM per device.

v0:
```python
import math
import jax
import jax.numpy as jnp
from jax import lax
from jax.sharding import PartitionSpec as P

TOPK = 8
CAP = 32
EPSILON = 1e-06


def from_behind(array, axis, by):
    size = lax.axis_size(axis)
    return lax.ppermute(array, axis, [(i, (i + by) % size) for i in range(size)])


def normalize(values):
    widened = values.astype(jnp.float32)
    factor = lax.rsqrt(jnp.mean(widened * widened, axis=-1, keepdims=True) + EPSILON)
    return (widened * factor, factor)


def slot_table(listed, window):
    hit_table = (listed[:, :, None] == jnp.arange(window, dtype=jnp.int32)[None, None, :]).astype(
        jnp.int32
    )
    flat_hits = hit_table.reshape(-1, window)
    before = jnp.cumsum(flat_hits, axis=0) - flat_hits
    ranked = jnp.sum(before * flat_hits, axis=1).reshape(listed.shape)
    return jnp.where(listed < window, listed * CAP + ranked, window * CAP)


def slot_owner(slot_ids, window):
    token_total = slot_ids.shape[0]
    token_index = jnp.repeat(jnp.arange(token_total, dtype=jnp.int32), slot_ids.shape[1])
    owners = (
        jnp.full((window * CAP + 1,), token_total, jnp.int32)
        .at[slot_ids.reshape(-1)]
        .set(token_index)
    )
    return owners[: window * CAP]


def slot_gates(slot_ids, gate_vals, window):
    filled = (
        jnp.zeros((window * CAP + 1,), jnp.float32)
        .at[slot_ids.reshape(-1)]
        .set(gate_vals.reshape(-1))
    )
    return filled[: window * CAP]


def pad_rows(row_table):
    extra = jnp.zeros((1, row_table.shape[-1]), row_table.dtype)
    return jnp.concatenate([row_table, extra], axis=0)


def local(
    section_input,
    saved_input,
    cotangent,
    routes_forward,
    gates_forward,
    routes_backward,
    gates_backward,
    gate_weight,
    up_weight,
    down_weight,
):
    window = lax.axis_size("expert")
    token_count = section_input.shape[1]
    model_width = section_input.shape[2]
    hidden_width = gate_weight.shape[3]
    gathered = (
        lax.all_gather(gate_weight, "dp", axis=2, tiled=True),
        lax.all_gather(up_weight, "dp", axis=2, tiled=True),
        lax.all_gather(down_weight, "dp", axis=2, tiled=True),
    )
    gate_full = gathered[0][0, 0]
    up_full = gathered[1][0, 0]
    down_full = gathered[2][0, 0]
    contract = (((1,), (1,)), ((), ()))
    normed, _ = normalize(section_input[0])
    slot_ids = slot_table(routes_forward[0], window)
    owners = slot_owner(slot_ids, window)
    sent_forward = pad_rows(normed.astype(jnp.bfloat16))[owners].reshape(window, CAP, model_width)
    saved_float, saved_scale = normalize(saved_input[0])
    back_slots = slot_table(routes_backward[0], window)
    back_owners = slot_owner(back_slots, window)
    back_gates = slot_gates(back_slots, gates_backward[0], window)
    sent_backward = pad_rows(saved_float.astype(jnp.bfloat16))[back_owners].reshape(
        window, CAP, model_width
    )
    grad_sent = (
        back_gates[:, None] * pad_rows(cotangent[0])[back_owners].astype(jnp.float32)
    ).astype(jnp.bfloat16)
    grad_sent = grad_sent.reshape(window, CAP, model_width)
    received = lax.all_to_all(sent_forward, "expert", split_axis=0, concat_axis=0, tiled=True)
    flat_rows = received.reshape(-1, model_width)
    gate_act = jnp.dot(flat_rows, gate_full, preferred_element_type=jnp.float32)
    up_act = jnp.dot(flat_rows, up_full, preferred_element_type=jnp.float32)
    hidden = (gate_act * jax.nn.sigmoid(gate_act) * up_act).astype(jnp.bfloat16)
    produced = jnp.dot(hidden, down_full, preferred_element_type=jnp.float32).astype(jnp.bfloat16)
    returned = lax.all_to_all(
        produced.reshape(received.shape), "expert", split_axis=0, concat_axis=0, tiled=True
    )
    received = (
        lax.all_to_all(sent_backward, "expert", split_axis=0, concat_axis=0, tiled=True),
        lax.all_to_all(grad_sent, "expert", split_axis=0, concat_axis=0, tiled=True),
    )
    received_rows = received[0]
    lead = received_rows.shape[:2]
    flat_rows = received_rows.reshape(-1, model_width)
    flat_grads = received[1].reshape(-1, model_width)
    gate_act = jnp.dot(flat_rows, gate_full, preferred_element_type=jnp.float32)
    up_act = jnp.dot(flat_rows, up_full, preferred_element_type=jnp.float32)
    sigma = jax.nn.sigmoid(gate_act)
    activated = gate_act * sigma
    hidden = (activated * up_act).astype(jnp.bfloat16)
    grad_hidden = lax.dot_general(
        flat_grads, down_full, contract, preferred_element_type=jnp.float32
    )
    grad_gate = (grad_hidden * up_act * sigma * (1.0 + gate_act * (1.0 - sigma))).astype(
        jnp.bfloat16
    )
    grad_up = (grad_hidden * activated).astype(jnp.bfloat16)
    grad_input = lax.dot_general(grad_gate, gate_full, contract, preferred_element_type=jnp.float32)
    grad_input = grad_input + lax.dot_general(
        grad_up, up_full, contract, preferred_element_type=jnp.float32
    )
    hidden, grad_gate, grad_up, grad_input = (
        hidden.reshape(lead + (hidden_width,)),
        grad_gate.reshape(lead + (hidden_width,)),
        grad_up.reshape(lead + (hidden_width,)),
        grad_input.astype(jnp.bfloat16).reshape(lead + (model_width,)),
    )
    sent_home = lax.all_to_all(grad_input, "expert", split_axis=0, concat_axis=0, tiled=True)
    grad_returned, expert_rows, expert_grads, hidden, grad_gate, grad_up = (
        sent_home,
        received[0],
        received[1],
        hidden,
        grad_gate,
        grad_up,
    )
    returned_pad = pad_rows(returned.reshape(window * CAP, model_width))
    mixed_sum = section_input[0].astype(jnp.float32)
    for slot_pos in range(TOPK):
        mixed_sum = mixed_sum + gates_forward[0][:, slot_pos, None] * returned_pad[
            slot_ids[:, slot_pos]
        ].astype(jnp.float32)
    handed = from_behind(mixed_sum.astype(jnp.bfloat16)[None], "section", 1)
    grad_pad = pad_rows(grad_returned.reshape(window * CAP, model_width))
    token_grad = jnp.zeros((token_count, model_width), jnp.float32)
    for slot_pos in range(TOPK):
        token_grad = token_grad + grad_pad[back_slots[:, slot_pos]].astype(jnp.float32)
    mean_term = jnp.mean(saved_float * token_grad, axis=-1, keepdims=True)
    input_grad = cotangent[0].astype(jnp.float32) + saved_scale * (
        token_grad - saved_float * mean_term
    )
    grad_back = from_behind(input_grad.astype(jnp.bfloat16)[None], "section", -1)
    rows_flat = expert_rows.reshape(-1, model_width)
    grads_flat = expert_grads.reshape(-1, model_width)
    hidden_flat = hidden.reshape(-1, hidden_width)
    gate_up = jnp.concatenate(
        [grad_gate.reshape(-1, hidden_width), grad_up.reshape(-1, hidden_width)], axis=1
    )
    transposed = (((0,), (0,)), ((), ()))
    left_part = rows_flat
    summed_in = lax.psum_scatter(
        lax.dot_general(left_part, gate_up, transposed, preferred_element_type=jnp.float32).astype(
            jnp.bfloat16
        ),
        "dp",
        scatter_dimension=0,
        tiled=True,
    ).astype(jnp.float32)
    left_part = hidden_flat
    summed_out = lax.psum_scatter(
        lax.dot_general(
            left_part, grads_flat, transposed, preferred_element_type=jnp.float32
        ).astype(jnp.bfloat16),
        "dp",
        scatter_dimension=0,
        tiled=True,
    ).astype(jnp.float32)
    grad_scale = 1.0 / math.sqrt(lax.axis_size("dp") * token_count)
    grad_gate_out = (summed_in[:, :hidden_width] * grad_scale)[None, None]
    grad_up_out = (summed_in[:, hidden_width:] * grad_scale)[None, None]
    grad_down_out = (summed_out * grad_scale)[None, None]
    return (handed, grad_back, grad_gate_out, grad_up_out, grad_down_out)


def solution(mesh):
    return jax.shard_map(
        local,
        mesh=mesh,
        in_specs=(
            P("section", ("dp", "expert"), None),
            P("section", ("dp", "expert"), None),
            P("section", ("dp", "expert"), None),
            P("section", ("dp", "expert"), None),
            P("section", ("dp", "expert"), None),
            P("section", ("dp", "expert"), None),
            P("section", ("dp", "expert"), None),
            P("section", "expert", "dp", None),
            P("section", "expert", "dp", None),
            P("section", "expert", "dp", None),
        ),
        out_specs=(
            P("section", ("dp", "expert"), None),
            P("section", ("dp", "expert"), None),
            P("section", "expert", "dp", None),
            P("section", "expert", "dp", None),
            P("section", "expert", "dp", None),
        ),
        check_vma=False,
    )
```

profile of v0, /device:TPU:2, one launch (start us, length us, event | category | flops | bytes accessed | tf_op | source)
XLA Modules:
  0.0 379.8 jit_solution(1343728989343063745)
XLA Ops:
  12.7 2.3 reduce-window.16
  15.9 4.3 %scatter_custom_fusion.2 = s32[257]{0:T(512)S(1)} fusion(s32[1024]{0:T(1024)S(1)} %bitcast.187, s32[1024]{0:T(1024)S(1)} %reshape.855, s32[]{:T(128)} %constant.17.clone.1), kind=kCustom, calls=%fused_computation.181 | custom fusion | bytes 1032 | tf_op jit(solution)/shard_map/scatter | solution.py:39
  20.2 2.0 gather_fusion.10
  22.2 4.5 %all-to-all-start.3 = ((bf16[8,32,1024]{2,1,0:T(8,128)(2,1)}), bf16[8,32,1024]{2,1,0:T(8,128)(2,1)S(1)}, u32[]{:S(2)}, u32[]{:S(2)}) async-start(bf16[8,32,1024]{2,1,0:T(8,128)(2,1)} %bitcast.37), calls=%async_computation.3 | async-start | bytes 1048576 | tf_op jit(solution)/shard_map/all_to_all | solution.py:108
  26.9 2.3 reduce-window.14
  31.1 4.3 %scatter_custom_fusion.1 = f32[257]{0:T(512)S(1)} fusion(s32[1024]{0:T(1024)S(1)} %bitcast.188, f32[1024]{0:T(1024)S(1)} %reshape.847, f32[]{:T(128)} %constant.13.clone.1), kind=kCustom, calls=%fused_computation.179 | custom fusion | bytes 1032 | tf_op jit(solution)/shard_map/scatter | solution.py:48
  37.0 4.4 %all-to-all-start.2 = ((bf16[8,32,1024]{2,1,0:T(8,128)(2,1)}), bf16[8,32,1024]{2,1,0:T(8,128)(2,1)S(1)}, u32[]{:S(2)}, u32[]{:S(2)}) async-start(bf16[8,32,1024]{2,1,0:T(8,128)(2,1)} %fusion.2), calls=%async_computation.2 | async-start | bytes 1048576 | tf_op jit(solution)/shard_map/all_to_all | solution.py:109
  41.4 43.9 %all-gather.4.cloned.1.call-done = bf16[1,1,1024,512]{3,2,1,0:T(8,128)(2,1)} async-done(((bf16[1,1,64,512]{3,2,1,0:T(8,128)(2,1)}), bf16[1,1,1024,512]{3,2,1,0:T(8,128)(2,1)}) %all-gather.4.cloned.1.call-update) | async-done | bytes 1048592 | tf_op jit(solution)/shard_map/all_gather | solution.py:75
  87.0 67.9 %all-gather.6.cloned.1.call-done = bf16[1,1,1024,512]{3,2,1,0:T(8,128)(2,1)} async-done(((bf16[1,1,64,512]{3,2,1,0:T(8,128)(2,1)}), bf16[1,1,1024,512]{3,2,1,0:T(8,128)(2,1)}) %all-gather.6.cloned.1.call-update) | async-done | bytes 1048592 | tf_op jit(solution)/shard_map/all_gather | solution.py:76
  158.6 4.3 %scatter_custom_fusion = s32[257]{0:T(512)S(1)} fusion(s32[1024]{0:T(1024)S(1)} %bitcast.189, s32[1024]{0:T(1024)S(1)} %reshape.855, s32[]{:T(128)} %constant.17.clone.1), kind=kCustom, calls=%fused_computation.183 | custom fusion | bytes 1032 | tf_op jit(solution)/shard_map/scatter | solution.py:39
  163.2 61.5 %all-gather.8.cloned.1.call-done = bf16[1,1,512,1024]{3,2,1,0:T(8,128)(2,1)} async-done(((bf16[1,1,32,1024]{3,2,1,0:T(8,128)(2,1)}), bf16[1,1,512,1024]{3,2,1,0:T(8,128)(2,1)}) %all-gather.8.cloned.1.call-update) | async-done | bytes 1048592 | tf_op jit(solution)/shard_map/all_gather | solution.py:77
  224.7 1.9 multiply_convert_fusion.1
  226.7 2.1 convolution_convert_fusion
  228.8 2.0 gather_fusion
  230.8 4.4 %all-to-all-start = ((bf16[8,32,1024]{2,1,0:T(8,128)(2,1)}), bf16[8,32,1024]{2,1,0:T(8,128)(2,1)S(1)}, u32[]{:S(2)}, u32[]{:S(2)}) async-start(bf16[8,32,1024]{2,1,0:T(8,128)(2,1)} %bitcast.6), calls=%async_computation | async-start | bytes 1048576 | tf_op jit(solution)/shard_map/all_to_all | solution.py:98
  240.0 5.5 %all-to-all-done = bf16[8,32,1024]{2,1,0:T(8,128)(2,1)S(1)} async-done(((bf16[8,32,1024]{2,1,0:T(8,128)(2,1)}), bf16[8,32,1024]{2,1,0:T(8,128)(2,1)S(1)}, u32[]{:S(2)}, u32[]{:S(2)}) %all-to-all-start) | async-done | bytes 524320 | tf_op jit(solution)/shard_map/all_to_all | solution.py:98
  246.8 3.0 convolution_convert_fusion.2
  249.8 3.7 all-to-all-start.1
  255.2 8.3 %all-to-all-done.1 = bf16[8,32,1024]{2,1,0:T(8,128)(2,1)S(1)} async-done(((bf16[8,32,1024]{2,1,0:T(8,128)(2,1)}), bf16[8,32,1024]{2,1,0:T(8,128)(2,1)S(1)}, u32[]{:S(2)}, u32[]{:S(2)}) %all-to-all-start.1) | async-done | bytes 524320 | tf_op jit(solution)/shard_map/all_to_all | solution.py:104
  263.5 3.5 all-to-all-start.4
  277.5 3.4 collective-permute-start
  289.3 2.5 collective-permute-start.1
  291.8 7.7 %collective-permute-done.1 = bf16[1,128,1024]{2,1,0:T(8,128)(2,1)S(1)} collective-permute-done((bf16[1,128,1024]{2,1,0:T(8,128)(2,1)S(1)}, bf16[1,128,1024]{2,1,0:T(8,128)(2,1)S(1)}, u32[]{:S(2)}, u32[]{:S(2)}) %collective-permute-start.1) | collective-permute-done | bytes 262176 | tf_op jit(solution)/shard_map/ppermute | solution.py:14
  301.0 69.2 %reduce-scatter.3.cloned.1.call-done = bf16[64,1024]{1,0:T(8,128)(2,1)} async-done(((bf16[1024,1024]{1,0:T(8,128)(2,1)}), bf16[64,1024]{1,0:T(8,128)(2,1)}) %reduce-scatter.3.cloned.1.call-update) | async-done | bytes 131088 | tf_op jit(solution)/shard_map/reduce_scatter | solution.py:170
  (146 shorter events, 46.5 us)
Async XLA Ops:
  7.2 78.2 %all-gather.4.cloned.1.call-start = ((), (), s32[]{:S(2)}) async-start(), calls=%async_computation.7 | async-start | bytes 1114112 | tf_op jit(solution)/shard_map/all_gather | solution.py:75
  7.9 147.0 %all-gather.6.cloned.1.call-start = ((), (), s32[]{:S(2)}) async-start(), calls=%async_computation.8 | async-start | bytes 1114112 | tf_op jit(solution)/shard_map/all_gather | solution.py:76
  8.6 216.1 %all-gather.8.cloned.1.call-start = ((), (), s32[]{:S(2)}) async-start(), calls=%async_computation.9 | async-start | bytes 1114112 | tf_op jit(solution)/shard_map/all_gather | solution.py:77
  11.6 3.9 %copy-start.7 = (f32[128]{0:T(128)}, f32[128]{0:T(128)S(1)}, u32[]{:S(2)}) copy-start(f32[128]{0:T(128)S(1)} %add_rsqrt_fusion) | copy-start | bytes 1540
  20.2 6.5 %copy-start.9 = (s32[1,128,8]{1,2,0:T(8,128)S(1)}, s32[1,128,8]{1,2,0:T(8,128)}, u32[]{:S(2)}) copy-start(s32[1,128,8]{1,2,0:T(8,128)} %param.13) | copy-start | bytes 12292
  20.2 9.5 %copy-start.4 = (bf16[1,128,1024]{2,1,0:T(8,128)(2,1)S(1)}, bf16[1,128,1024]{2,1,0:T(8,128)(2,1)}, u32[]{:S(2)}) copy-start(bf16[1,128,1024]{2,1,0:T(8,128)(2,1)} %param.12) | copy-start | bytes 786436
  22.2 14.8 %all-to-all-start.3 = ((bf16[8,32,1024]{2,1,0:T(8,128)(2,1)}), bf16[8,32,1024]{2,1,0:T(8,128)(2,1)S(1)}, u32[]{:S(2)}, u32[]{:S(2)}) async-start(bf16[8,32,1024]{2,1,0:T(8,128)(2,1)} %bitcast.37), calls=%async_computation.3 | async-start | bytes 1048576 | tf_op jit(solution)/shard_map/all_to_all | solution.py:108
  37.0 119.6 %all-to-all-start.2 = ((bf16[8,32,1024]{2,1,0:T(8,128)(2,1)}), bf16[8,32,1024]{2,1,0:T(8,128)(2,1)S(1)}, u32[]{:S(2)}, u32[]{:S(2)}) async-start(bf16[8,32,1024]{2,1,0:T(8,128)(2,1)} %fusion.2), calls=%async_computation.2 | async-start | bytes 1048576 | tf_op jit(solution)/shard_map/all_to_all | solution.py:109
  41.3 258.2 %reduce-scatter.5.cloned.1.call-start = ((), (), s32[]{:S(2)}) async-start(), calls=%async_computation.11 | async-start | bytes 1114112 | tf_op jit(solution)/shard_map/reduce_scatter | solution.py:179
  156.6 6.5 %copy-start.6 = (f32[256,512]{1,0:T(8,128)}, f32[256,512]{1,0:T(8,128)S(1)}, u32[]{:S(2)}) copy-start(f32[256,512]{1,0:T(8,128)S(1)} %fusion.7) | copy-start | bytes 1572868
  156.6 6.3 %copy-start.3 = (bf16[1,128,1024]{2,1,0:T(8,128)(2,1)S(1)}, bf16[1,128,1024]{2,1,0:T(8,128)(2,1)}, u32[]{:S(2)}) copy-start(bf16[1,128,1024]{2,1,0:T(8,128)(2,1)} %param.10) | copy-start | bytes 786436
  158.1 212.0 %reduce-scatter.3.cloned.1.call-start = ((), (), s32[]{:S(2)}) async-start(), calls=%async_computation.10 | async-start | bytes 2228224 | tf_op jit(solution)/shard_map/reduce_scatter | solution.py:170
  230.8 14.7 %copy-start = (bf16[1,1,1024,512]{3,2,1,0:T(8,128)(2,1)S(1)}, bf16[1,1,1024,512]{3,2,1,0:T(8,128)(2,1)}, u32[]{:S(2)}) copy-start(bf16[1,1,1024,512]{3,2,1,0:T(8,128)(2,1)} %all-gather.4.cloned.1.call-done) | copy-start | bytes 3145732
  230.8 16.0 %copy-start.1 = (bf16[1,1,1024,512]{3,2,1,0:T(8,128)(2,1)S(1)}, bf16[1,1,1024,512]{3,2,1,0:T(8,128)(2,1)}, u32[]{:S(2)}) copy-start(bf16[1,1,1024,512]{3,2,1,0:T(8,128)(2,1)} %all-gather.6.cloned.1.call-done) | copy-start | bytes 3145732
  230.8 14.7 %all-to-all-start = ((bf16[8,32,1024]{2,1,0:T(8,128)(2,1)}), bf16[8,32,1024]{2,1,0:T(8,128)(2,1)S(1)}, u32[]{:S(2)}, u32[]{:S(2)}) async-start(bf16[8,32,1024]{2,1,0:T(8,128)(2,1)} %bitcast.6), calls=%async_computation | async-start | bytes 1048576 | tf_op jit(solution)/shard_map/all_to_all | solution.py:98
  249.8 13.7 %all-to-all-start.1 = ((bf16[8,32,1024]{2,1,0:T(8,128)(2,1)}), bf16[8,32,1024]{2,1,0:T(8,128)(2,1)S(1)}, u32[]{:S(2)}, u32[]{:S(2)}) async-start(bf16[8,32,1024]{2,1,0:T(8,128)(2,1)} %bitcast.181), calls=%async_computation.1 | async-start | bytes 1048576 | tf_op jit(solution)/shard_map/all_to_all | solution.py:104
  263.5 17.4 %all-to-all-start.4 = ((bf16[8,32,1024]{2,1,0:T(8,128)(2,1)}), bf16[8,32,1024]{2,1,0:T(8,128)(2,1)S(1)}, u32[]{:S(2)}, u32[]{:S(2)}) async-start(bf16[8,32,1024]{2,1,0:T(8,128)(2,1)} %bitcast.39), calls=%async_computation.4 | async-start | bytes 1048576 | tf_op jit(solution)/shard_map/all_to_all | solution.py:137
  274.2 2.0 copy-start.11
  274.2 2.0 copy-start.12
  274.2 2.0 copy-start.13
  277.5 14.3 %collective-permute-start = (bf16[1,128,1024]{2,1,0:T(8,128)(2,1)}, bf16[1,128,1024]{2,1,0:T(8,128)(2,1)S(1)}, u32[]{:S(2)}, u32[]{:S(2)}) collective-permute-start(bf16[1,128,1024]{2,1,0:T(8,128)(2,1)} %fusion.33), channel_id=1, source_target_pairs={{0,128},{128,256},{256,384},{384,0},{1,129},{129,257},{257,385},{3... | collective-permute-start | bytes 786440 | tf_op jit(solution)/shard_map/ppermute | solution.py:14
  286.3 2.3 copy-start.2
  286.3 2.3 copy-start.8
  289.3 10.2 %collective-permute-start.1 = (bf16[1,128,1024]{2,1,0:T(8,128)(2,1)S(1)}, bf16[1,128,1024]{2,1,0:T(8,128)(2,1)S(1)}, u32[]{:S(2)}, u32[]{:S(2)}) collective-permute-start(bf16[1,128,1024]{2,1,0:T(8,128)(2,1)S(1)} %fusion.39), channel_id=1, source_target_pairs={{0,384},{128,0},{256,128},{384,256},{1,385},{129,1},{257,129},{385... | collective-permute-start | bytes 786440 | tf_op jit(solution)/shard_map/ppermute | solution.py:14
  (7 other events, 13.0 us)
Sparse Core Ops, SparseCore 0:
  10.1 75.2 all-gather.3
  87.4 67.4 all-gather.5
  157.0 67.6 all-gather.7
  227.4 68.3 reduce-scatter.4
  298.5 71.6 reduce-scatter.2
where the time goes:
time: 381 us; the launch traced here: 380 us
  waiting for transfers between devices  267 us (70%)
  local copies, waits for them, and re-layouts  39.5 us (10%)
  starting transfers between devices  26.4 us (7%)
  other arithmetic  17.9 us (5%)
  matrix products  14.8 us (4%)
  between operations  14.4 us (4%)
    reduce_scatter x1, waiting for transfers between devices, local(): lax.psum_scatter(lax.dot_general(left_part, gate_up, transposed, preferre...  69.2 us
    all_gather x1, waiting for transfers between devices, local(): lax.all_gather(up_weight, 'dp', axis=2, tiled=True)  67.9 us
    all_gather x1, waiting for transfers between devices, local(): lax.all_gather(down_weight, 'dp', axis=2, tiled=True)  61.5 us
    all_gather x1, waiting for transfers between devices, local(): lax.all_gather(gate_weight, 'dp', axis=2, tiled=True)  43.9 us
    scatter x2, local copies, waits for them, and re-layouts, slot_owner(): owners = jnp.full((window * CAP + 1,), token_total, jnp.int32).at[slot_id...  8.61 us
    all_to_all x1, waiting for transfers between devices, local(): lax.all_to_all(produced.reshape(received.shape), 'expert', split_axis=0,...  8.33 us
    gather x8, local copies, waits for them, and re-layouts, local(): returned_pad[slot_ids[:, slot_pos]].astype(jnp.float32)  7.86 us
    ppermute x2, waiting for transfers between devices, from_behind(): lax.ppermute(array, axis, [(i, (i + by) % size) for i in range(size)])  7.75 us
  transfers between devices with their start and end apart: 12, of which 8 were waited for; matrix products, arithmetic and copies ran while one was open for 18% of the time, Pallas kernels for 0%

commit v1 on v0

--- a/solution.py
+++ b/solution.py
@@ -7,6 +7,13 @@
 TOPK = 8
 CAP = 32
 EPSILON = 1e-06
+
+
+def swapped_in(block, name, d):
+    size = lax.axis_size(name)
+    tiles = jnp.stack([block for _ in range(size)])
+    tiles = lax.all_to_all(tiles, name, split_axis=0, concat_axis=0)
+    return jnp.concatenate(tiles, axis=d)
 
 
 def from_behind(array, axis, by):
@@ -73,7 +80,7 @@
     hidden_width = gate_weight.shape[3]
     gathered = (
         lax.all_gather(gate_weight, "dp", axis=2, tiled=True),
-        lax.all_gather(up_weight, "dp", axis=2, tiled=True),
+        swapped_in(up_weight, "dp", 2),
         lax.all_gather(down_weight, "dp", axis=2, tiled=True),
     )
     gate_full = gathered[0][0, 0]

time: 381 us -> 361 us (0.948)
  waiting for transfers between devices: 267 us -> 228 us
  blocking collectives: 0 us -> 14.6 us
  starting transfers between devices: 26.4 us -> 36.3 us
    all_gather x1 -> x0, waiting for transfers between devices: 67.9 us -> none  [local(): lax.all_gather(up_weight, 'dp', axis=2, tiled=True)]
    all_to_all x1, waiting for transfers between devices: 0.43 us -> 41.5 us  [swapped_in(): tiles = lax.all_to_all(tiles, name, split_axis=0, concat_axis=0)]
    all_gather x1, waiting for transfers between devices: 43.9 us -> 28.5 us  [local(): lax.all_gather(gate_weight, 'dp', axis=2, tiled=True)]
    all_to_all x0 -> x1, blocking collectives: none -> 14.6 us  [local(): lax.all_to_all(sent_backward, 'expert', split_axis=0, concat_axis=0, tile...]
    all_to_all x1, starting transfers between devices: 4.47 us -> 15.2 us  [swapped_in(): tiles = lax.all_to_all(tiles, name, split_axis=0, concat_axis=0)]
    all_to_all x1, waiting for transfers between devices: 5.54 us -> 9.47 us  [local(): lax.all_to_all(sent_forward, 'expert', split_axis=0, concat_axis=0, tiled...]
  transfers between devices with their start and end apart: 12 -> 11, of which waited for: 8 -> 7; matrix products, arithmetic and copies ran while one was open for 18% -> 14% of each run, Pallas kernels for 0% -> 0%
where the time goes in v1:
time: 361 us; the launch traced here: 360 us
  waiting for transfers between devices  228 us (63%)
  local copies, waits for them, and re-layouts  36.4 us (10%)
  starting transfers between devices  36.3 us (10%)
  matrix products  15.7 us (4%)
  blocking collectives  14.6 us (4%)
  other arithmetic  14.4 us (4%)
  between operations  14.3 us (4%)
    reduce_scatter x1, waiting for transfers between devices, local(): lax.psum_scatter(lax.dot_general(left_part, gate_up, transposed, preferre...  72.1 us
    all_gather x1, waiting for transfers between devices, local(): lax.all_gather(down_weight, 'dp', axis=2, tiled=True)  59.1 us
    all_to_all x1, waiting for transfers between devices, swapped_in(): tiles = lax.all_to_all(tiles, name, split_axis=0, concat_axis=0)  41.5 us
    all_gather x1, waiting for transfers between devices, local(): lax.all_gather(gate_weight, 'dp', axis=2, tiled=True)  28.5 us
    all_to_all x1, starting transfers between devices, swapped_in(): tiles = lax.all_to_all(tiles, name, split_axis=0, concat_axis=0)  15.2 us
    all_to_all x1, blocking collectives, local(): lax.all_to_all(sent_backward, 'expert', split_axis=0, concat_axis=0, tile...  14.6 us
    all_to_all x1, waiting for transfers between devices, local(): lax.all_to_all(sent_forward, 'expert', split_axis=0, concat_axis=0, tiled...  9.47 us
    scatter x2, local copies, waits for them, and re-layouts, slot_owner(): owners = jnp.full((window * CAP + 1,), token_total, jnp.int32).at[slot_id...  8.61 us
  transfers between devices with their start and end apart: 11, of which 7 were waited for; matrix products, arithmetic and copies ran while one was open for 14% of the time, Pallas kernels for 0%

profile of v1, /device:TPU:2, one launch (start us, length us, event | category | flops | bytes accessed | tf_op | source)
XLA Modules:
  0.0 359.9 jit_solution(8022468386849708122)
XLA Ops:
  10.4 2.3 reduce-window.16
  13.6 4.3 %scatter_custom_fusion.2 = s32[257]{0:T(512)S(1)} fusion(s32[1024]{0:T(1024)S(1)} %bitcast.189, s32[1024]{0:T(1024)S(1)} %reshape.858, s32[]{:T(128)} %constant.17.clone.1), kind=kCustom, calls=%fused_computation.177 | custom fusion | bytes 1032 | tf_op jit(solution)/shard_map/scatter | solution.py:46
  19.2 14.6 %all_to_all.30 = bf16[8,32,1024]{2,1,0:T(8,128)(2,1)S(1)} all-to-all(bf16[8,32,1024]{2,1,0:T(8,128)(2,1)S(1)} %bitcast.174), channel_id=1, replica_groups=mesh['section'=4,'dp'=16,'expert'=8] {'expert'}, dimensions={0} | all-to-all | bytes 1048576 | tf_op jit(solution)/shard_map/all_to_all | solution.py:115
  34.9 15.2 %all-to-all-start.1 = ((bf16[16,1,1,64,512]{4,3,2,1,0:T(8,128)(2,1)}), bf16[16,1,1,64,512]{4,3,2,1,0:T(8,128)(2,1)S(1)}, u32[]{:S(2)}, u32[]{:S(2)}) async-start(bf16[16,1,1,64,512]{4,3,2,1,0:T(8,128)(2,1)} %stack.2), calls=%async_computation.1 | async-start | bytes 2097152 | tf_op jit(solution)/shard_map/all_to_all | solution.py:15
  51.9 2.3 reduce-window.14
  56.0 4.3 %scatter_custom_fusion.1 = f32[257]{0:T(512)S(1)} fusion(s32[1024]{0:T(1024)S(1)} %bitcast.190, f32[1024]{0:T(1024)S(1)} %reshape.850, f32[]{:T(128)} %constant.13.clone.1), kind=kCustom, calls=%fused_computation.175 | custom fusion | bytes 1032 | tf_op jit(solution)/shard_map/scatter | solution.py:55
  61.5 41.5 %all-to-all-done.1 = bf16[16,1,1,64,512]{4,3,2,1,0:T(8,128)(2,1)S(1)} async-done(((bf16[16,1,1,64,512]{4,3,2,1,0:T(8,128)(2,1)}), bf16[16,1,1,64,512]{4,3,2,1,0:T(8,128)(2,1)S(1)}, u32[]{:S(2)}, u32[]{:S(2)}) %all-to-all-start.1) | async-done | bytes 1048608 | tf_op jit(solution)/shard_map/all_to_all | solution.py:15
  102.9 3.5 all-to-all-start.3
  106.5 28.5 %all-gather.3.cloned.1.call-done = bf16[1,1,1024,512]{3,2,1,0:T(8,128)(2,1)} async-done(((bf16[1,1,64,512]{3,2,1,0:T(8,128)(2,1)}), bf16[1,1,1024,512]{3,2,1,0:T(8,128)(2,1)}) %all-gather.3.cloned.1.call-update) | async-done | bytes 1048592 | tf_op jit(solution)/shard_map/all_gather | solution.py:82
  137.9 2.6 convolution_convert_fusion.1
  140.9 4.3 %scatter_custom_fusion = s32[257]{0:T(512)S(1)} fusion(s32[1024]{0:T(1024)S(1)} %bitcast.191, s32[1024]{0:T(1024)S(1)} %reshape.858, s32[]{:T(128)} %constant.17.clone.1), kind=kCustom, calls=%fused_computation.179 | custom fusion | bytes 1032 | tf_op jit(solution)/shard_map/scatter | solution.py:46
  145.5 59.1 %all-gather.5.cloned.1.call-done = bf16[1,1,512,1024]{3,2,1,0:T(8,128)(2,1)} async-done(((bf16[1,1,32,1024]{3,2,1,0:T(8,128)(2,1)}), bf16[1,1,512,1024]{3,2,1,0:T(8,128)(2,1)}) %all-gather.5.cloned.1.call-update) | async-done | bytes 1048592 | tf_op jit(solution)/shard_map/all_gather | solution.py:84
  204.6 2.1 multiply_convert_fusion.1
  206.7 2.1 convolution_convert_fusion
  210.8 4.4 %all-to-all-start = ((bf16[8,32,1024]{2,1,0:T(8,128)(2,1)}), bf16[8,32,1024]{2,1,0:T(8,128)(2,1)S(1)}, u32[]{:S(2)}, u32[]{:S(2)}) async-start(bf16[8,32,1024]{2,1,0:T(8,128)(2,1)} %bitcast.6), calls=%async_computation | async-start | bytes 1048576 | tf_op jit(solution)/shard_map/all_to_all | solution.py:105
  216.1 9.5 %all-to-all-done = bf16[8,32,1024]{2,1,0:T(8,128)(2,1)S(1)} async-done(((bf16[8,32,1024]{2,1,0:T(8,128)(2,1)}), bf16[8,32,1024]{2,1,0:T(8,128)(2,1)S(1)}, u32[]{:S(2)}, u32[]{:S(2)}) %all-to-all-start) | async-done | bytes 524320 | tf_op jit(solution)/shard_map/all_to_all | solution.py:105
  226.8 3.0 convolution_convert_fusion.2
  229.8 3.7 %all-to-all-start.2 = ((bf16[8,32,1024]{2,1,0:T(8,128)(2,1)}), bf16[8,32,1024]{2,1,0:T(8,128)(2,1)S(1)}, u32[]{:S(2)}, u32[]{:S(2)}) async-start(bf16[8,32,1024]{2,1,0:T(8,128)(2,1)} %bitcast.182), calls=%async_computation.2 | async-start | bytes 1048576 | tf_op jit(solution)/shard_map/all_to_all | solution.py:111
  235.2 8.5 %all-to-all-done.2 = bf16[8,32,1024]{2,1,0:T(8,128)(2,1)S(1)} async-done(((bf16[8,32,1024]{2,1,0:T(8,128)(2,1)}), bf16[8,32,1024]{2,1,0:T(8,128)(2,1)S(1)}, u32[]{:S(2)}, u32[]{:S(2)}) %all-to-all-start.2) | async-done | bytes 524320 | tf_op jit(solution)/shard_map/all_to_all | solution.py:111
  243.7 3.5 all-to-all-start.5
  255.4 3.4 collective-permute-start
  266.4 2.5 collective-permute-start.1
  268.9 7.7 %collective-permute-done.1 = bf16[1,128,1024]{2,1,0:T(8,128)(2,1)S(1)} collective-permute-done((bf16[1,128,1024]{2,1,0:T(8,128)(2,1)S(1)}, bf16[1,128,1024]{2,1,0:T(8,128)(2,1)S(1)}, u32[]{:S(2)}, u32[]{:S(2)}) %collective-permute-start.1) | collective-permute-done | bytes 262176 | tf_op jit(solution)/shard_map/ppermute | solution.py:21
  278.2 72.1 %reduce-scatter.3.cloned.1.call-done = bf16[64,1024]{1,0:T(8,128)(2,1)} async-done(((bf16[1024,1024]{1,0:T(8,128)(2,1)}), bf16[64,1024]{1,0:T(8,128)(2,1)}) %reduce-scatter.3.cloned.1.call-update) | async-done | bytes 131088 | tf_op jit(solution)/shard_map/reduce_scatter | solution.py:177
  (127 shorter events, 40.8 us)
Async XLA Ops:
  18.0 15.8 %copy-start.6 = (bf16[1,1,64,512]{3,2,1,0:T(8,128)(2,1)S(1)}, bf16[1,1,64,512]{3,2,1,0:T(8,128)(2,1)}, u32[]{:S(2)}) copy-start(bf16[1,1,64,512]{3,2,1,0:T(8,128)(2,1)} %param.18) | copy-start | bytes 196612
  19.2 32.4 %copy-start.7 = (s32[1,128,8]{1,2,0:T(8,128)S(1)}, s32[1,128,8]{1,2,0:T(8,128)}, u32[]{:S(2)}) copy-start(s32[1,128,8]{1,2,0:T(8,128)} %param.13) | copy-start | bytes 12292
  33.8 20.8 %copy-start.3 = (bf16[1,128,1024]{2,1,0:T(8,128)(2,1)S(1)}, bf16[1,128,1024]{2,1,0:T(8,128)(2,1)}, u32[]{:S(2)}) copy-start(bf16[1,128,1024]{2,1,0:T(8,128)(2,1)} %param.12) | copy-start | bytes 786436
  34.9 68.1 %all-to-all-start.1 = ((bf16[16,1,1,64,512]{4,3,2,1,0:T(8,128)(2,1)}), bf16[16,1,1,64,512]{4,3,2,1,0:T(8,128)(2,1)S(1)}, u32[]{:S(2)}, u32[]{:S(2)}) async-start(bf16[16,1,1,64,512]{4,3,2,1,0:T(8,128)(2,1)} %stack.2), calls=%async_computation.1 | async-start | bytes 2097152 | tf_op jit(solution)/shard_map/all_to_all | solution.py:15
  50.1 84.9 %all-gather.3.cloned.1.call-start = ((), (), s32[]{:S(2)}) async-start(), calls=%async_computation.8 | async-start | bytes 1114112 | tf_op jit(solution)/shard_map/all_gather | solution.py:82
  50.8 153.8 %all-gather.5.cloned.1.call-start = ((), (), s32[]{:S(2)}) async-start(), calls=%async_computation.9 | async-start | bytes 1114112 | tf_op jit(solution)/shard_map/all_gather | solution.py:84
  54.6 1.2 copy-start.8
  102.9 35.0 %all-to-all-start.3 = ((bf16[8,32,1024]{2,1,0:T(8,128)(2,1)}), bf16[8,32,1024]{2,1,0:T(8,128)(2,1)S(1)}, u32[]{:S(2)}, u32[]{:S(2)}) async-start(bf16[8,32,1024]{2,1,0:T(8,128)(2,1)} %fusion.2), calls=%async_computation.3 | async-start | bytes 1048576 | tf_op jit(solution)/shard_map/all_to_all | solution.py:116
  106.4 170.2 %reduce-scatter.5.cloned.1.call-start = ((), (), s32[]{:S(2)}) async-start(), calls=%async_computation.11 | async-start | bytes 1114112 | tf_op jit(solution)/shard_map/reduce_scatter | solution.py:186
  136.6 3.9 %copy-start.5 = (f32[256,512]{1,0:T(8,128)}, f32[256,512]{1,0:T(8,128)S(1)}, u32[]{:S(2)}) copy-start(f32[256,512]{1,0:T(8,128)S(1)} %fusion.8) | copy-start | bytes 1572868
  137.9 7.4 %copy-start.2 = (bf16[1,128,1024]{2,1,0:T(8,128)(2,1)S(1)}, bf16[1,128,1024]{2,1,0:T(8,128)(2,1)}, u32[]{:S(2)}) copy-start(bf16[1,128,1024]{2,1,0:T(8,128)(2,1)} %param.10) | copy-start | bytes 786436
  140.5 209.8 %reduce-scatter.3.cloned.1.call-start = ((), (), s32[]{:S(2)}) async-start(), calls=%async_computation.10 | async-start | bytes 2228224 | tf_op jit(solution)/shard_map/reduce_scatter | solution.py:177
  210.8 5.2 %copy-start.9 = (f32[1,128,8]{1,2,0:T(8,128)S(1)}, f32[1,128,8]{1,2,0:T(8,128)}, u32[]{:S(2)}) copy-start(f32[1,128,8]{1,2,0:T(8,128)} %param.14) | copy-start | bytes 12292
  210.8 14.7 %copy-start = (bf16[1,1,1024,512]{3,2,1,0:T(8,128)(2,1)S(1)}, bf16[1,1,1024,512]{3,2,1,0:T(8,128)(2,1)}, u32[]{:S(2)}) copy-start(bf16[1,1,1024,512]{3,2,1,0:T(8,128)(2,1)} %all-gather.3.cloned.1.call-done) | copy-start | bytes 3145732
  210.8 14.7 %all-to-all-start = ((bf16[8,32,1024]{2,1,0:T(8,128)(2,1)}), bf16[8,32,1024]{2,1,0:T(8,128)(2,1)S(1)}, u32[]{:S(2)}, u32[]{:S(2)}) async-start(bf16[8,32,1024]{2,1,0:T(8,128)(2,1)} %bitcast.6), calls=%async_computation | async-start | bytes 1048576 | tf_op jit(solution)/shard_map/all_to_all | solution.py:105
  229.8 13.9 %all-to-all-start.2 = ((bf16[8,32,1024]{2,1,0:T(8,128)(2,1)}), bf16[8,32,1024]{2,1,0:T(8,128)(2,1)S(1)}, u32[]{:S(2)}, u32[]{:S(2)}) async-start(bf16[8,32,1024]{2,1,0:T(8,128)(2,1)} %bitcast.182), calls=%async_computation.2 | async-start | bytes 1048576 | tf_op jit(solution)/shard_map/all_to_all | solution.py:111
  243.7 15.0 %all-to-all-start.5 = ((bf16[8,32,1024]{2,1,0:T(8,128)(2,1)}), bf16[8,32,1024]{2,1,0:T(8,128)(2,1)S(1)}, u32[]{:S(2)}, u32[]{:S(2)}) async-start(bf16[8,32,1024]{2,1,0:T(8,128)(2,1)} %bitcast.40), calls=%async_computation.5 | async-start | bytes 1048576 | tf_op jit(solution)/shard_map/all_to_all | solution.py:144
  255.4 13.5 %collective-permute-start = (bf16[1,128,1024]{2,1,0:T(8,128)(2,1)}, bf16[1,128,1024]{2,1,0:T(8,128)(2,1)S(1)}, u32[]{:S(2)}, u32[]{:S(2)}) collective-permute-start(bf16[1,128,1024]{2,1,0:T(8,128)(2,1)} %fusion.28), channel_id=1, source_target_pairs={{0,128},{128,256},{256,384},{384,0},{1,129},{129,257},{257,385},{3... | collective-permute-start | bytes 786440 | tf_op jit(solution)/shard_map/ppermute | solution.py:21
  264.0 1.7 copy-start.1
  264.9 1.3 copy-start.4
  266.4 10.2 %collective-permute-start.1 = (bf16[1,128,1024]{2,1,0:T(8,128)(2,1)S(1)}, bf16[1,128,1024]{2,1,0:T(8,128)(2,1)S(1)}, u32[]{:S(2)}, u32[]{:S(2)}) collective-permute-start(bf16[1,128,1024]{2,1,0:T(8,128)(2,1)S(1)} %fusion.34), channel_id=1, source_target_pairs={{0,384},{128,0},{256,128},{384,256},{1,385},{129,1},{257,129},{385... | collective-permute-start | bytes 786440 | tf_op jit(solution)/shard_map/ppermute | solution.py:21
Sparse Core Ops, SparseCore 0:
  53.0 81.9 all-gather.2
  137.1 67.4 all-gather.4
  207.4 68.3 reduce-scatter.4
  278.5 71.7 reduce-scatter.2
